TPU v7x, 256 devices: a whole 4x4x8 slice. The times are simulated.
256 devices in a mesh: rows: 8 (over y_hi, x), cols: 32 (over y_lo, z, core).
Axes of the slice: x: 4, y: 4 (y_hi: 2, y_lo: 2; y = y_hi * 2 + y_lo), z: 8, core: 2. Of those that a mesh axis runs over, the one named last changes fastest.
Arguments:
- coarse_one: bfloat16 [64, 2048, 128], P('rows', 'cols'), may hold values from -100 to 100
- coarse_two: bfloat16 [64, 2048, 128], P('rows', 'cols'), may hold values from -100 to 100
- fine_one: bfloat16 [128, 4096, 128], P('rows', 'cols'), may hold values from -100 to 100
- fine_two: bfloat16 [128, 4096, 128], P('rows', 'cols'), may hold values from -100 to 100
- selection: int32 [8, 32, 12, 32], P('rows', 'cols'), may hold values from 0 to 1, as said below
- counts: int32 [8, 32], P('rows', 'cols'), may hold values from 1 to 12, as said below
Outputs:
- coarse_flow: float32 [2, 64, 2048], P(None, 'rows', 'cols')
- refined_flow: float32 [2, 128, 4096], P(None, 'rows', 'cols')
Inputs may be any that keep to these rules, and one draw needn't show every extreme that they name: `selection`: each slot row is one-hot; slot 0 of tile (r, c) names its own panel c; the first counts[r, c] slots name distinct panels; later slots name arbitrary panels. `counts`: some tile has 12 valid slots.
All inputs are finite; a program needn't handle non-finite values.
Results may differ from a plain program's by a relative error of at most 0.0003.
Values may be sent and summed in bfloat16 or wider, within the bound.
A program may use at most 128 MiB of HBM per device.

v0:
```python
import functools

import jax
import jax.numpy as jnp
import numpy as np
from jax import lax
from jax.experimental import pallas as pl
from jax.experimental.pallas import tpu as pltpu
from jax.sharding import PartitionSpec as P

MESH = pl.DeviceIdType.MESH
F32 = jnp.float32
BF16 = jnp.bfloat16
NROWS, NCOLS = 8, 32
NZ = 8
CH = 128
BH, BW = 8, 64
FH, FW = 16, 128
RAD = 4
PAD = 8
SCALE = float(np.log2(np.e) / np.sqrt(128.0))
LOW = -1.0e30
NEIGHBOURS = [(dy, dx) for dy in (-1, 0, 1) for dx in (-1, 0, 1) if (dy, dx) != (0, 0)]
NT = (((1,), (1,)), ((), ()))


def spans(d, size, halo):
    if d == 0:
        return 0, size, halo
    if d == 1:
        return size - halo, halo, 0
    return 0, halo, size + halo


def kernel(
    c1, c2, f1, f2, sel, cnt,
    coarse_out, fine_out,
    kb, qb, f1v, ext, wbuf, maskb, pscr, lv, biasb, acc, st_tx, st_rx, fl, ft,
    ring_send, ring_recv, q_send, q_recv, lv_send, lv_recv, halo_send, halo_recv,
    st_send, st_recv, fl_send, fl_recv, loc,
):
    r = lax.axis_index("rows")
    c = lax.axis_index("cols")
    ylo = c // 16
    z = (c // 2) % NZ
    core = c % 2

    def at_z(zz):
        return (r, ylo * 16 + zz * 2 + core)

    ring_to = (at_z((z + 1) % NZ), at_z((z + NZ - 1) % NZ))

    def partner(j):
        return (r, ((ylo + j // 2) % 2) * 16 + z * 2 + (core + j % 2) % 2)

    def neighbour(dy, dx):
        return ((r + dy + NROWS) % NROWS, (c + dx + NCOLS) % NCOLS)

    everyone = list(ring_to) + [partner(j) for j in (1, 2, 3)] + [neighbour(*n) for n in NEIGHBOURS]

    own_k = pltpu.make_async_copy(c2, kb.at[0:2], loc.at[0])
    own_q = pltpu.make_async_copy(c1, qb.at[0], loc.at[1])
    own_f1 = pltpu.make_async_copy(f1, f1v, loc.at[2])
    own_f2 = pltpu.make_async_copy(f2, ext.at[RAD : RAD + FH, PAD : PAD + FW], loc.at[3])
    for copy in (own_k, own_q, own_f1, own_f2):
        copy.start()

    slot = lax.broadcasted_iota(jnp.int32, (12, NCOLS), 0)
    chosen = jnp.where(slot < cnt[...], sel[0, 0], 0)
    live = jnp.sum(chosen.astype(F32), axis=0, keepdims=True)
    lv[0] = jnp.broadcast_to(jnp.concatenate([live, jnp.zeros((1, 128 - NCOLS), F32)], axis=1), (8, 128))

    barrier = pltpu.get_barrier_semaphore()
    for device in everyone:
        pl.semaphore_signal(barrier, inc=1, device_id=device, device_id_type=MESH)
    pl.semaphore_wait(barrier, len(everyone))

    def ring(way, d, h, source):
        return pltpu.make_async_remote_copy(
            src_ref=source, dst_ref=kb.at[2 + (d * 2 + h) * 2 + way],
            send_sem=ring_send.at[way, d, h], recv_sem=ring_recv.at[way, d, h],
            device_id=ring_to[way], device_id_type=MESH,
        )

    for h in range(2):
        for way in range(2):
            ring(way, 0, h, c2.at[h]).start()

    def share(j, source, target, send, recv):
        return pltpu.make_async_remote_copy(
            src_ref=source, dst_ref=target, send_sem=send.at[j - 1], recv_sem=recv.at[j - 1],
            device_id=partner(j), device_id_type=MESH,
        )

    lives = [share(j, lv.at[0], lv.at[j], lv_send, lv_recv) for j in (1, 2, 3)]
    asks = [share(j, c1, qb.at[j], q_send, q_recv) for j in (1, 2, 3)]
    for copy in asks + lives:
        copy.start()

    halos = []
    for i, (dy, dx) in enumerate(NEIGHBOURS):
        ys, yn, yt = spans(dy, FH, RAD)
        xs, xn, xt = spans(dx, FW, PAD)
        halos.append(
            pltpu.make_async_remote_copy(
                src_ref=f2.at[ys : ys + yn, xs : xs + xn], dst_ref=ext.at[yt : yt + yn, xt : xt + xn],
                send_sem=halo_send.at[i], recv_sem=halo_recv.at[i],
                device_id=neighbour(dy, dx), device_id_type=MESH,
            )
        )
    for copy in halos:
        copy.start()

    key = lax.broadcasted_iota(jnp.int32, (512, 128), 0)
    query = lax.broadcasted_iota(jnp.int32, (512, 128), 1)
    off_y = key // 32 - RAD - query // 16
    off_x = key % 32 - PAD - query % 16
    inside = (jnp.abs(off_y) <= RAD) & (jnp.abs(off_x) <= RAD)
    maskb[...] = jnp.where(inside, 0.0, LOW)

    for j in range(4):
        acc[j, 0] = jnp.full((8, 512), LOW, F32)
        for s in (1, 2, 3):
            acc[j, s] = jnp.zeros((8, 512), F32)

    def set_bias(j):
        lane = lax.broadcasted_iota(jnp.int32, (NCOLS, 128), 1)
        panel = lax.broadcasted_iota(jnp.int32, (NCOLS, 128), 0)
        column = jnp.sum(jnp.where(lane == panel, lv[j][0:1, :], 0.0), axis=1, keepdims=True)
        biasb[j] = jnp.broadcast_to((1.0 - column) * (2.0 * LOW), (NCOLS, 256))

    set_bias(0)
    own_k.wait()
    own_q.wait()
    own_f1.wait()
    own_f2.wait()
    for copy in asks + lives:
        copy.wait_recv()
    for j in (1, 2, 3):
        set_bias(j)

    def match(at, panel, h):
        keys = kb[at].reshape(4 * BW, CH)
        base = (panel * BW).astype(F32)
        first_row = (h * 4).astype(F32)

        def tile(i, _):
            j, half = i // 2, i % 2
            lanes = pl.ds(pl.multiple_of(half * 256, 256), 256)
            queries = qb[j, half].reshape(256, CH)
            score = lax.dot_general(keys, queries, NT, preferred_element_type=F32)
            score = score.reshape(4, 8, 8, 256)
            top = jnp.max(score, axis=(0, 1))
            weight = jnp.exp2((score - top) * SCALE)
            by_row = [functools.reduce(jnp.add, [weight[y, v] for v in range(8)]) for y in range(4)]
            by_col = [functools.reduce(jnp.add, [weight[y, v] for y in range(4)]) for v in range(8)]
            total = (by_row[0] + by_row[1]) + (by_row[2] + by_row[3])
            in_row = by_row[1] + 2.0 * by_row[2] + 3.0 * by_row[3] + first_row * total
            in_col = functools.reduce(jnp.add, [(8.0 * v) * by_col[v] for v in range(1, 8)]) + base * total
            seen = top + biasb[j, pl.ds(panel, 1), :]
            before = acc[j, 0, :, lanes]
            now = jnp.maximum(before, seen)
            keep = jnp.exp2((before - now) * SCALE)
            take = jnp.exp2((seen - now) * SCALE)
            acc[j, 0, :, lanes] = now
            acc[j, 1, :, lanes] = keep * acc[j, 1, :, lanes] + take * total
            acc[j, 2, :, lanes] = keep * acc[j, 2, :, lanes] + take * in_col
            acc[j, 3, :, lanes] = keep * acc[j, 3, :, lanes] + take * in_row
            return 0

        lax.fori_loop(0, 8, tile, 0)

    def window(b):
        by, bx = b // 8, b % 8
        rows = pl.ds(by * 8, 16)
        keys = ext[rows, pl.ds(pl.multiple_of(bx * 16, 16), 32), :].reshape(512, CH)
        queries = f1v[pl.ds(by * 8, 8), pl.ds(pl.multiple_of(bx * 16, 16), 16), :].reshape(128, CH)
        score = lax.dot_general(keys, queries, NT, preferred_element_type=F32) + maskb[...]
        top = jnp.max(score, axis=0, keepdims=True)
        weight = jnp.exp2((score - top) * SCALE)
        total = jnp.sum(weight, axis=0, keepdims=True)
        pairs = weight.reshape(8, 2, 32, 128)
        pairs = (pairs[:, 0] + pairs[:, 1]) * (1.0 / total)
        pscr[...] = pairs.reshape(256, 128)
        wbuf[b] = pscr[pl.ds(0, 128, stride=2), :] + pscr[pl.ds(1, 128, stride=2), :]

    def step(t, _):
        d, h = (t + 1) // 2 - 1, (t + 1) % 2

        @pl.when(t >= 1)
        def _():
            for way in range(2):

                @pl.when((d < 3) | (h == way))
                def _():
                    ring(way, d, h, kb.at[0]).wait_recv()

                    @pl.when((d < 2) | ((d == 2) & (h == way)))
                    def _():
                        ring(way, d + 1, h, kb.at[2 + (d * 2 + h) * 2 + way]).start()

        def chunk(way, _):
            own = t == 0

            @pl.when(own | (d < 3) | (h == way))
            def _():
                zs = jnp.where(own, z, (z + NZ + (2 * way - 1) * (d + 1)) % NZ)
                match(2 * t + way, ylo * 16 + zs * 2 + core, jnp.where(own, way, h))

            return 0

        lax.fori_loop(0, 2, chunk, 0)

        @pl.when(t == 1)
        def _():
            for copy in halos:
                copy.wait_recv()

            @pl.when(r == 0)
            def _():
                ext[0:RAD] = jnp.zeros((RAD, FW + 2 * PAD, CH), BF16)

            @pl.when(r == NROWS - 1)
            def _():
                ext[RAD + FH :] = jnp.zeros((RAD, FW + 2 * PAD, CH), BF16)

            @pl.when(c == 0)
            def _():
                ext[:, 0:PAD] = jnp.zeros((FH + 2 * RAD, PAD, CH), BF16)

            @pl.when(c == NCOLS - 1)
            def _():
                ext[:, PAD + FW :] = jnp.zeros((FH + 2 * RAD, PAD, CH), BF16)

        @pl.when(t >= 1)
        def _():
            window(2 * t - 2)
            window(2 * t - 1)

        return 0

    lax.fori_loop(0, 9, step, 0)

    sub = lax.broadcasted_iota(jnp.int32, (8, 512), 0).astype(F32)

    def moments(j):
        top8, total, in_col, in_row = acc[j, 0], acc[j, 1], acc[j, 2], acc[j, 3]
        in_col = in_col + sub * total
        top = jnp.max(top8, axis=0, keepdims=True)
        part = jnp.exp2((top8 - top) * SCALE)
        sums = [jnp.sum(part * v, axis=0, keepdims=True) for v in (total, in_col, in_row)]
        return jnp.concatenate([top] + sums + [jnp.zeros((4, 512), F32)], axis=0)

    backs = [share(j, st_tx.at[j - 1], st_rx.at[j - 1], st_send, st_recv) for j in (1, 2, 3)]
    for j in (3, 2, 1):
        st_tx[j - 1] = moments(j)
        backs[j - 1].start()
    parts = [moments(0)]
    for j in (1, 2, 3):
        backs[j - 1].wait_recv()
        parts.append(st_rx[j - 1])
    top = functools.reduce(jnp.maximum, [p[0:1] for p in parts])
    scales = [jnp.exp2((p[0:1] - top) * SCALE) for p in parts]
    total, in_col, in_row = (
        functools.reduce(jnp.add, [s * p[i : i + 1] for s, p in zip(scales, parts)]) for i in (1, 2, 3)
    )
    cell = lax.broadcasted_iota(jnp.int32, (1, 512), 1)
    query_col = (c * BW + cell % BW).astype(F32)
    query_row = (cell // BW).astype(F32)
    flow_x = (in_col / total - query_col) * (1.0 / 256.0)
    flow_y = (in_row / total - query_row) * (1.0 / 256.0)
    flow = jnp.concatenate([f[:, 128 * i : 128 * i + 128] for f in (flow_x, flow_y) for i in range(4)], axis=0)
    fl[1, 1] = flow
    coarse_out[...] = flow
    edges = []
    for i, (dy, dx) in enumerate(NEIGHBOURS):
        edges.append(
            pltpu.make_async_remote_copy(
                src_ref=fl.at[1, 1], dst_ref=fl.at[1 - dy, 1 - dx],
                send_sem=fl_send.at[i], recv_sem=fl_recv.at[i],
                device_id=neighbour(dy, dx), device_id_type=MESH,
            )
        )
    for copy in edges:
        copy.start()
    for copy in edges:
        copy.wait_recv()

    tiles = {}
    for ty in range(3):
        for tx in range(3):
            tile = fl[ty, tx]
            outside = []
            if ty == 0:
                outside.append(r == 0)
            if ty == 2:
                outside.append(r == NROWS - 1)
            if tx == 0:
                outside.append(c == 0)
            if tx == 2:
                outside.append(c == NCOLS - 1)
            for gone in outside:
                tile = tile * jnp.where(gone, 0.0, 1.0)
            tiles[ty, tx] = tile

    i72 = lax.broadcasted_iota(jnp.int32, (72, 128), 0)
    lane = lax.broadcasted_iota(jnp.int32, (72, 128), 1)
    goal = jnp.where(i72 < 4, 60 + i72, jnp.where(i72 < 68, i72 - 4, i72 - 68))
    for e in range(12):
        ty = 0 if e < 2 else (1 if e < 10 else 2)
        row = (e - 2) % 8
        hit = lane == goal + (row % 2) * 64
        for k in range(2):
            at = k * 4 + row // 2
            left, mid, right = (tiles[ty, tx][at : at + 1, :] for tx in range(3))
            pick = jnp.where(i72 < 4, left, jnp.where(i72 < 68, mid, right))
            ft[k, e] = jnp.broadcast_to(
                jnp.sum(jnp.where(hit, pick, 0.0), axis=1, keepdims=True), (72, 128)
            )

    for b in range(16):
        by, bx = b // 8, b % 8
        weight = wbuf[b].reshape(8, 16, 128)
        for k in range(2):
            value = ft[k, by * 4 : by * 4 + 8, bx * 8 : bx * 8 + 16, :]
            fine_out[k, b : b + 1, :] = jnp.sum((weight * value).reshape(128, 128), axis=0, keepdims=True)

    for h in range(2):
        for way in range(2):
            for d in range(4):
                if d < 3 or h == way:
                    ring(way, d, h, kb.at[0]).wait_send()
    for copy in asks + lives + halos + backs + edges:
        copy.wait_send()


def local(coarse_one, coarse_two, fine_one, fine_two, selection, counts):
    vm = pltpu.VMEM
    dma = pltpu.SemaphoreType.DMA
    any_spec = pl.BlockSpec(memory_space=pl.ANY)
    vm_spec = pl.BlockSpec(memory_space=pltpu.VMEM)
    coarse, fine = pl.pallas_call(
        kernel,
        out_shape=(jax.ShapeDtypeStruct((8, 128), F32), jax.ShapeDtypeStruct((2, 16, 128), F32)),
        in_specs=[any_spec] * 4 + [vm_spec] * 2,
        out_specs=(vm_spec, vm_spec),
        scratch_shapes=[
            vm((18, 4, BW, CH), BF16),
            vm((4, 2, 4, BW, CH), BF16),
            vm((FH, FW, CH), BF16),
            vm((FH + 2 * RAD, FW + 2 * PAD, CH), BF16),
            vm((16, 128, 128), F32),
            vm((512, 128), F32),
            vm((256, 128), F32),
            vm((4, 8, 128), F32),
            vm((4, NCOLS, 256), F32),
            vm((4, 4, 8, 512), F32),
            vm((3, 8, 512), F32),
            vm((3, 8, 512), F32),
            vm((3, 3, 8, 128), F32),
            vm((2, 12, 72, 128), F32),
            dma((2, 4, 2)), dma((2, 4, 2)),
            dma((3,)), dma((3,)), dma((3,)), dma((3,)),
            dma((8,)), dma((8,)),
            dma((3,)), dma((3,)),
            dma((8,)), dma((8,)),
            dma((4,)),
        ],
        compiler_params=pltpu.CompilerParams(collective_id=0, has_side_effects=True, vmem_limit_bytes=48 << 20),
        name="flow",
    )(
        coarse_one.reshape(2, 4, BW, CH), coarse_two.reshape(2, 4, BW, CH), fine_one, fine_two, selection, counts
    )
    coarse = coarse.reshape(2, BH, BW)
    fine = fine.reshape(2, 2, 8, 8, 16).transpose(0, 1, 3, 2, 4).reshape(2, FH, FW)
    return coarse, fine


def solution(mesh):
    return jax.shard_map(
        local,
        mesh=mesh,
        in_specs=(
            P("rows", "cols", None),
            P("rows", "cols", None),
            P("rows", "cols", None),
            P("rows", "cols", None),
            P("rows", "cols", None, None),
            P("rows", "cols"),
        ),
        out_specs=(P(None, "rows", "cols"), P(None, "rows", "cols")),
        check_vma=False,
    )
```

profile of v0, /device:TPU:1, one launch (start us, length us, event | category | flops | bytes accessed | tf_op | source)
XLA Modules:
  0.0 74.9 jit_solution(306880761013283650)
XLA Ops:
  0.6 0.7 copy.8.sel
  2.0 0.0 copy-start
  2.0 1.0 %copy-done = bf16[16,128,128]{2,1,0:T(8,128)(2,1)S(1)} copy-done((bf16[16,128,128]{2,1,0:T(8,128)(2,1)S(1)}, bf16[16,128,128]{2,1,0:T(8,128)(2,1)}, u32[]{:S(2)}) %copy-start) | copy-done | bytes 524312
  3.0 0.0 copy-start.1
  3.0 1.0 %copy-done.1 = bf16[16,128,128]{2,1,0:T(8,128)(2,1)S(1)} copy-done((bf16[16,128,128]{2,1,0:T(8,128)(2,1)S(1)}, bf16[16,128,128]{2,1,0:T(8,128)(2,1)}, u32[]{:S(2)}) %copy-start.1) | copy-done | bytes 524312
  4.1 0.0 copy-start.2
  4.1 0.9 %copy-done.2 = bf16[8,64,128]{2,1,0:T(8,128)(2,1)S(1)} copy-done((bf16[8,64,128]{2,1,0:T(8,128)(2,1)S(1)}, bf16[8,64,128]{2,1,0:T(8,128)(2,1)}, u32[]{:S(2)}) %copy-start.2) | copy-done | bytes 131096
  5.0 0.0 copy-start.3
  5.0 0.9 %copy-done.3 = bf16[8,64,128]{2,1,0:T(8,128)(2,1)S(1)} copy-done((bf16[8,64,128]{2,1,0:T(8,128)(2,1)S(1)}, bf16[8,64,128]{2,1,0:T(8,128)(2,1)}, u32[]{:S(2)}) %copy-start.3) | copy-done | bytes 131096
  5.9 67.5 %flow.1 = (f32[8,128]{1,0:T(8,128)S(1)}, f32[2,16,128]{2,1,0:T(8,128)S(1)}) custom-call(bf16[2,4,64,128]{3,2,1,0:T(8,128)(2,1)S(1)} %bitcast.5, bf16[2,4,64,128]{3,2,1,0:T(8,128)(2,1)S(1)} %bitcast.6, bf16[16,128,128]{2,1,0:T(8,128)(2,1)S(1)} %copy-done, bf16[16,128,128]{2,1,0:T(8,128)(2,1)S(1)} %copy-done.1, s32[1,1,12,32]{3,2,1,0:T(8,128)S(1)} %copy.8.sel, ...), custom_call_target="tpu_custom_call" | custom-call | tf_op jit(solution)/shard_map/flow/pallas_call | solution.py:342
  73.4 0.1 reshape.22
  73.5 0.7 reshape.23
  74.2 0.7 reshape.21
  (1 shorter events, 0.0 us)
Async XLA Ops:
  2.0 1.0 %copy-start = (bf16[16,128,128]{2,1,0:T(8,128)(2,1)S(1)}, bf16[16,128,128]{2,1,0:T(8,128)(2,1)}, u32[]{:S(2)}) copy-start(bf16[16,128,128]{2,1,0:T(8,128)(2,1)} %f1.1) | copy-start | bytes 1572868
  3.0 1.0 %copy-start.1 = (bf16[16,128,128]{2,1,0:T(8,128)(2,1)S(1)}, bf16[16,128,128]{2,1,0:T(8,128)(2,1)}, u32[]{:S(2)}) copy-start(bf16[16,128,128]{2,1,0:T(8,128)(2,1)} %f2.1) | copy-start | bytes 1572868
  4.1 0.9 %copy-start.2 = (bf16[8,64,128]{2,1,0:T(8,128)(2,1)S(1)}, bf16[8,64,128]{2,1,0:T(8,128)(2,1)}, u32[]{:S(2)}) copy-start(bf16[8,64,128]{2,1,0:T(8,128)(2,1)} %param.6) | copy-start | bytes 393220
  5.0 0.9 %copy-start.3 = (bf16[8,64,128]{2,1,0:T(8,128)(2,1)S(1)}, bf16[8,64,128]{2,1,0:T(8,128)(2,1)}, u32[]{:S(2)}) copy-start(bf16[8,64,128]{2,1,0:T(8,128)(2,1)} %param.7) | copy-start | bytes 393220
where the time goes:
time: 75.1 us; the launch traced here: 74.9 us
  Pallas kernels  67.5 us (90%)
  local copies, waits for them, and re-layouts  6.07 us (8%)
  between operations  1.32 us (2%)
    pallas_call x1, Pallas kernels, local(): pl.pallas_call(kernel, out_shape=(jax.ShapeDtypeStruct((8, 128), F32), ja...  67.5 us
    unnamed x9, local copies, waits for them, and re-layouts  4.58 us

commit v1 on v0

--- a/solution.py
+++ b/solution.py
@@ -35,7 +35,7 @@
 def kernel(
     c1, c2, f1, f2, sel, cnt,
     coarse_out, fine_out,
-    kb, qb, f1v, ext, wbuf, maskb, pscr, lv, biasb, acc, st_tx, st_rx, fl, ft,
+    kb, qb, q2, f1v, ext, wbuf, maskb, pscr, selv, cntv, lv, biasb, acc, st_tx, st_rx, fl, ft,
     ring_send, ring_recv, q_send, q_recv, lv_send, lv_recv, halo_send, halo_recv,
     st_send, st_recv, fl_send, fl_recv, loc,
 ):
@@ -56,19 +56,51 @@
     def neighbour(dy, dx):
         return ((r + dy + NROWS) % NROWS, (c + dx + NCOLS) % NCOLS)
 
+    def exists(dy, dx):
+        there = True
+        for d, at, last in ((dy, r, NROWS - 1), (dx, c, NCOLS - 1)):
+            if d == -1:
+                there = there & (at > 0)
+            if d == 1:
+                there = there & (at < last)
+        return there
+
+    def each(copies, what):
+        for copy, (dy, dx) in zip(copies, NEIGHBOURS):
+            there = exists(-dy, -dx) if what == "wait_recv" else exists(dy, dx)
+
+            @pl.when(there)
+            def _(copy=copy):
+                getattr(copy, what)()
+
     everyone = list(ring_to) + [partner(j) for j in (1, 2, 3)] + [neighbour(*n) for n in NEIGHBOURS]
 
-    own_k = pltpu.make_async_copy(c2, kb.at[0:2], loc.at[0])
+    own_sel = pltpu.make_async_copy(sel, selv, loc.at[4])
+    own_cnt = pltpu.make_async_copy(cnt, cntv, loc.at[5])
+    own_k = pltpu.make_async_copy(c2, kb.at[0], loc.at[0])
     own_q = pltpu.make_async_copy(c1, qb.at[0], loc.at[1])
     own_f1 = pltpu.make_async_copy(f1, f1v, loc.at[2])
     own_f2 = pltpu.make_async_copy(f2, ext.at[RAD : RAD + FH, PAD : PAD + FW], loc.at[3])
-    for copy in (own_k, own_q, own_f1, own_f2):
+    for copy in (own_sel, own_cnt, own_k, own_q, own_f1, own_f2):
         copy.start()
 
-    slot = lax.broadcasted_iota(jnp.int32, (12, NCOLS), 0)
-    chosen = jnp.where(slot < cnt[...], sel[0, 0], 0)
-    live = jnp.sum(chosen.astype(F32), axis=0, keepdims=True)
-    lv[0] = jnp.broadcast_to(jnp.concatenate([live, jnp.zeros((1, 128 - NCOLS), F32)], axis=1), (8, 128))
+    fl[...] = jnp.zeros((3, 3, 8, 128), F32)
+
+    @pl.when(r == 0)
+    def _():
+        ext[0:RAD] = jnp.zeros((RAD, FW + 2 * PAD, CH), BF16)
+
+    @pl.when(r == NROWS - 1)
+    def _():
+        ext[RAD + FH :] = jnp.zeros((RAD, FW + 2 * PAD, CH), BF16)
+
+    @pl.when(c == 0)
+    def _():
+        ext[:, 0:PAD] = jnp.zeros((FH + 2 * RAD, PAD, CH), BF16)
+
+    @pl.when(c == NCOLS - 1)
+    def _():
+        ext[:, PAD + FW :] = jnp.zeros((FH + 2 * RAD, PAD, CH), BF16)
 
     barrier = pltpu.get_barrier_semaphore()
     for device in everyone:
@@ -77,7 +109,7 @@
 
     def ring(way, d, h, source):
         return pltpu.make_async_remote_copy(
-            src_ref=source, dst_ref=kb.at[2 + (d * 2 + h) * 2 + way],
+            src_ref=source, dst_ref=kb.at[jnp.minimum(1 + 2 * d + way, 7), h],
             send_sem=ring_send.at[way, d, h], recv_sem=ring_recv.at[way, d, h],
             device_id=ring_to[way], device_id_type=MESH,
         )
@@ -94,7 +126,17 @@
 
     lives = [share(j, lv.at[0], lv.at[j], lv_send, lv_recv) for j in (1, 2, 3)]
     asks = [share(j, c1, qb.at[j], q_send, q_recv) for j in (1, 2, 3)]
-    for copy in asks + lives:
+    for copy in asks:
+        copy.start()
+
+    own_sel.wait()
+    own_cnt.wait()
+    slot = lax.broadcasted_iota(jnp.int32, (12, 1, NCOLS), 0)
+    chosen = jnp.where(slot < cntv[...].reshape(1, 1, 1), selv[...], 0)
+    live = jnp.sum(chosen.astype(F32), axis=0)
+    lv[0] = jnp.broadcast_to(jnp.concatenate([live, jnp.zeros((1, 128 - NCOLS), F32)], axis=1), (8, 128))
+
+    for copy in lives:
         copy.start()
 
     halos = []
@@ -108,8 +150,7 @@
                 device_id=neighbour(dy, dx), device_id_type=MESH,
             )
         )
-    for copy in halos:
-        copy.start()
+    each(halos, "start")
 
     key = lax.broadcasted_iota(jnp.int32, (512, 128), 0)
     query = lax.broadcasted_iota(jnp.int32, (512, 128), 1)
@@ -129,46 +170,49 @@
         column = jnp.sum(jnp.where(lane == panel, lv[j][0:1, :], 0.0), axis=1, keepdims=True)
         biasb[j] = jnp.broadcast_to((1.0 - column) * (2.0 * LOW), (NCOLS, 256))
 
+    def split(j):
+        q = qb[j].reshape(BH * BW, CH).astype(F32) * SCALE
+        high = q.astype(BF16)
+        q2[j] = jnp.concatenate([high, (q - high.astype(F32)).astype(BF16)], axis=1)
+
     set_bias(0)
+    own_q.wait()
+    split(0)
     own_k.wait()
-    own_q.wait()
     own_f1.wait()
     own_f2.wait()
-    for copy in asks + lives:
-        copy.wait_recv()
     for j in (1, 2, 3):
+        lives[j - 1].wait_recv()
         set_bias(j)
-
-    def match(at, panel, h):
-        keys = kb[at].reshape(4 * BW, CH)
+        asks[j - 1].wait_recv()
+        split(j)
+
+    def match(at, panel):
+        keys = kb[at].reshape(BH * BW, CH)
+        keys = jnp.concatenate([keys, keys], axis=1)
         base = (panel * BW).astype(F32)
-        first_row = (h * 4).astype(F32)
-
-        def tile(i, _):
-            j, half = i // 2, i % 2
-            lanes = pl.ds(pl.multiple_of(half * 256, 256), 256)
-            queries = qb[j, half].reshape(256, CH)
-            score = lax.dot_general(keys, queries, NT, preferred_element_type=F32)
-            score = score.reshape(4, 8, 8, 256)
-            top = jnp.max(score, axis=(0, 1))
-            weight = jnp.exp2((score - top) * SCALE)
-            by_row = [functools.reduce(jnp.add, [weight[y, v] for v in range(8)]) for y in range(4)]
-            by_col = [functools.reduce(jnp.add, [weight[y, v] for y in range(4)]) for v in range(8)]
-            total = (by_row[0] + by_row[1]) + (by_row[2] + by_row[3])
-            in_row = by_row[1] + 2.0 * by_row[2] + 3.0 * by_row[3] + first_row * total
-            in_col = functools.reduce(jnp.add, [(8.0 * v) * by_col[v] for v in range(1, 8)]) + base * total
-            seen = top + biasb[j, pl.ds(panel, 1), :]
-            before = acc[j, 0, :, lanes]
-            now = jnp.maximum(before, seen)
-            keep = jnp.exp2((before - now) * SCALE)
-            take = jnp.exp2((seen - now) * SCALE)
-            acc[j, 0, :, lanes] = now
-            acc[j, 1, :, lanes] = keep * acc[j, 1, :, lanes] + take * total
-            acc[j, 2, :, lanes] = keep * acc[j, 2, :, lanes] + take * in_col
-            acc[j, 3, :, lanes] = keep * acc[j, 3, :, lanes] + take * in_row
-            return 0
-
-        lax.fori_loop(0, 8, tile, 0)
+        for j in range(4):
+            for lanes in (pl.ds(0, 256), pl.ds(256, 256)):
+                score = lax.dot_general(keys, q2[j, lanes, :], NT, preferred_element_type=F32)
+                score = score.reshape(64, 8, 256)
+                top = jnp.max(score, axis=0)
+                level = [jnp.exp2(score[i] - top) for i in range(64)]
+                odd = []
+                while len(level) > 1:
+                    odd.append(functools.reduce(jnp.add, level[1::2]))
+                    level = [a + b for a, b in zip(level[0::2], level[1::2])]
+                total = level[0]
+                in_col = 8.0 * (odd[0] + 2.0 * odd[1] + 4.0 * odd[2]) + base * total
+                in_row = odd[3] + 2.0 * odd[4] + 4.0 * odd[5]
+                seen = top + biasb[j, pl.ds(panel, 1), :]
+                before = acc[j, 0, :, lanes]
+                now = jnp.maximum(before, seen)
+                keep = jnp.exp2(before - now)
+                take = jnp.exp2(seen - now)
+                acc[j, 0, :, lanes] = now
+                acc[j, 1, :, lanes] = keep * acc[j, 1, :, lanes] + take * total
+                acc[j, 2, :, lanes] = keep * acc[j, 2, :, lanes] + take * in_col
+                acc[j, 3, :, lanes] = keep * acc[j, 3, :, lanes] + take * in_row
 
     def window(b):
         by, bx = b // 8, b % 8
@@ -184,62 +228,37 @@
         pscr[...] = pairs.reshape(256, 128)
         wbuf[b] = pscr[pl.ds(0, 128, stride=2), :] + pscr[pl.ds(1, 128, stride=2), :]
 
-    def step(t, _):
-        d, h = (t + 1) // 2 - 1, (t + 1) % 2
-
-        @pl.when(t >= 1)
+    def ready_windows():
+        each(halos, "wait_recv")
+
+    def two_windows(i, _):
+        window(2 * i)
+        window(2 * i + 1)
+        return 0
+
+    def step(p, _):
+        @pl.when(p < 6)
+        def _():
+            d, h = p // 2, p % 2
+            for way in range(2):
+                ring(way, d, h, kb.at[0, 0]).wait_recv()
+
+                @pl.when((d < 2) | (h == way))
+                def _(way=way):
+                    ring(way, d + 1, h, kb.at[1 + 2 * d + way, h]).start()
+
+        @pl.when(p == 7)
         def _():
             for way in range(2):
-
-                @pl.when((d < 3) | (h == way))
-                def _():
-                    ring(way, d, h, kb.at[0]).wait_recv()
-
-                    @pl.when((d < 2) | ((d == 2) & (h == way)))
-                    def _():
-                        ring(way, d + 1, h, kb.at[2 + (d * 2 + h) * 2 + way]).start()
-
-        def chunk(way, _):
-            own = t == 0
-
-            @pl.when(own | (d < 3) | (h == way))
-            def _():
-                zs = jnp.where(own, z, (z + NZ + (2 * way - 1) * (d + 1)) % NZ)
-                match(2 * t + way, ylo * 16 + zs * 2 + core, jnp.where(own, way, h))
-
-            return 0
-
-        lax.fori_loop(0, 2, chunk, 0)
-
-        @pl.when(t == 1)
-        def _():
-            for copy in halos:
-                copy.wait_recv()
-
-            @pl.when(r == 0)
-            def _():
-                ext[0:RAD] = jnp.zeros((RAD, FW + 2 * PAD, CH), BF16)
-
-            @pl.when(r == NROWS - 1)
-            def _():
-                ext[RAD + FH :] = jnp.zeros((RAD, FW + 2 * PAD, CH), BF16)
-
-            @pl.when(c == 0)
-            def _():
-                ext[:, 0:PAD] = jnp.zeros((FH + 2 * RAD, PAD, CH), BF16)
-
-            @pl.when(c == NCOLS - 1)
-            def _():
-                ext[:, PAD + FW :] = jnp.zeros((FH + 2 * RAD, PAD, CH), BF16)
-
-        @pl.when(t >= 1)
-        def _():
-            window(2 * t - 2)
-            window(2 * t - 1)
-
+                ring(way, 3, way, kb.at[0, 0]).wait_recv()
+
+        depth = (p + 1) // 2
+        sign = jnp.where(p == 7, -1, 1 - 2 * (p % 2))
+        zs = (z + NZ + sign * depth) % NZ
+        match(p, ylo * 16 + zs * 2 + core)
         return 0
 
-    lax.fori_loop(0, 9, step, 0)
+    lax.fori_loop(0, 8, step, 0)
 
     sub = lax.broadcasted_iota(jnp.int32, (8, 512), 0).astype(F32)
 
@@ -247,7 +266,7 @@
         top8, total, in_col, in_row = acc[j, 0], acc[j, 1], acc[j, 2], acc[j, 3]
         in_col = in_col + sub * total
         top = jnp.max(top8, axis=0, keepdims=True)
-        part = jnp.exp2((top8 - top) * SCALE)
+        part = jnp.exp2(top8 - top)
         sums = [jnp.sum(part * v, axis=0, keepdims=True) for v in (total, in_col, in_row)]
         return jnp.concatenate([top] + sums + [jnp.zeros((4, 512), F32)], axis=0)
 
@@ -256,11 +275,13 @@
         st_tx[j - 1] = moments(j)
         backs[j - 1].start()
     parts = [moments(0)]
+    ready_windows()
+    lax.fori_loop(0, 4, two_windows, 0)
     for j in (1, 2, 3):
         backs[j - 1].wait_recv()
         parts.append(st_rx[j - 1])
     top = functools.reduce(jnp.maximum, [p[0:1] for p in parts])
-    scales = [jnp.exp2((p[0:1] - top) * SCALE) for p in parts]
+    scales = [jnp.exp2(p[0:1] - top) for p in parts]
     total, in_col, in_row = (
         functools.reduce(jnp.add, [s * p[i : i + 1] for s, p in zip(scales, parts)]) for i in (1, 2, 3)
     )
@@ -281,27 +302,14 @@
                 device_id=neighbour(dy, dx), device_id_type=MESH,
             )
         )
-    for copy in edges:
-        copy.start()
-    for copy in edges:
-        copy.wait_recv()
+    each(edges, "start")
+    lax.fori_loop(4, 8, two_windows, 0)
+    each(edges, "wait_recv")
 
     tiles = {}
     for ty in range(3):
         for tx in range(3):
-            tile = fl[ty, tx]
-            outside = []
-            if ty == 0:
-                outside.append(r == 0)
-            if ty == 2:
-                outside.append(r == NROWS - 1)
-            if tx == 0:
-                outside.append(c == 0)
-            if tx == 2:
-                outside.append(c == NCOLS - 1)
-            for gone in outside:
-                tile = tile * jnp.where(gone, 0.0, 1.0)
-            tiles[ty, tx] = tile
+            tiles[ty, tx] = fl[ty, tx]
 
     i72 = lax.broadcasted_iota(jnp.int32, (72, 128), 0)
     lane = lax.broadcasted_iota(jnp.int32, (72, 128), 1)
@@ -329,9 +337,11 @@
         for way in range(2):
             for d in range(4):
                 if d < 3 or h == way:
-                    ring(way, d, h, kb.at[0]).wait_send()
-    for copy in asks + lives + halos + backs + edges:
+                    ring(way, d, h, kb.at[0, 0]).wait_send()
+    for copy in asks + lives + backs:
         copy.wait_send()
+    each(halos, "wait_send")
+    each(edges, "wait_send")
 
 
 def local(coarse_one, coarse_two, fine_one, fine_two, selection, counts):
@@ -342,16 +352,19 @@
     coarse, fine = pl.pallas_call(
         kernel,
         out_shape=(jax.ShapeDtypeStruct((8, 128), F32), jax.ShapeDtypeStruct((2, 16, 128), F32)),
-        in_specs=[any_spec] * 4 + [vm_spec] * 2,
+        in_specs=[any_spec] * 5 + [pl.BlockSpec(memory_space=pltpu.HBM)],
         out_specs=(vm_spec, vm_spec),
         scratch_shapes=[
-            vm((18, 4, BW, CH), BF16),
+            vm((8, 2, 4, BW, CH), BF16),
             vm((4, 2, 4, BW, CH), BF16),
+            vm((4, BH * BW, 2 * CH), BF16),
             vm((FH, FW, CH), BF16),
             vm((FH + 2 * RAD, FW + 2 * PAD, CH), BF16),
             vm((16, 128, 128), F32),
             vm((512, 128), F32),
             vm((256, 128), F32),
+            vm((12, 1, NCOLS), jnp.int32),
+            vm((1, 1), jnp.int32),
             vm((4, 8, 128), F32),
             vm((4, NCOLS, 256), F32),
             vm((4, 4, 8, 512), F32),
@@ -364,12 +377,13 @@
             dma((8,)), dma((8,)),
             dma((3,)), dma((3,)),
             dma((8,)), dma((8,)),
-            dma((4,)),
+            dma((6,)),
         ],
-        compiler_params=pltpu.CompilerParams(collective_id=0, has_side_effects=True, vmem_limit_bytes=48 << 20),
+        compiler_params=pltpu.CompilerParams(collective_id=0, has_side_effects=True, vmem_limit_bytes=63 << 20),
         name="flow",
     )(
-        coarse_one.reshape(2, 4, BW, CH), coarse_two.reshape(2, 4, BW, CH), fine_one, fine_two, selection, counts
+        coarse_one.reshape(2, 4, BW, CH), coarse_two.reshape(2, 4, BW, CH), fine_one, fine_two,
+        selection.reshape(12, 1, NCOLS), counts
     )
     coarse = coarse.reshape(2, BH, BW)
     fine = fine.reshape(2, 2, 8, 8, 16).transpose(0, 1, 3, 2, 4).reshape(2, FH, FW)

time: 75.1 us -> 47.3 us (0.63)
  Pallas kernels: 67.5 us -> 43.6 us
  local copies, waits for them, and re-layouts: 6.07 us -> 2.21 us
    pallas_call x1, Pallas kernels: 67.5 us -> 43.6 us  [local(): pl.pallas_call(kernel, out_shape=(jax.ShapeDtypeStruct((8, 128), F32), ja...]
    unnamed x9 -> x2, local copies, waits for them, and re-layouts: 4.58 us -> 0.01 us
where the time goes in v1:
time: 47.3 us; the launch traced here: 47.1 us
  Pallas kernels  43.6 us (92%)
  local copies, waits for them, and re-layouts  2.21 us (5%)
  between operations  1.31 us (3%)
    pallas_call x1, Pallas kernels, local(): pl.pallas_call(kernel, out_shape=(jax.ShapeDtypeStruct((8, 128), F32), ja...  43.6 us
    reshape x2, local copies, waits for them, and re-layouts, local(): fine.reshape(2, 2, 8, 8, 16).transpose(0, 1, 3, 2, 4).reshape(2, FH, FW)  1.51 us

profile of v1, /device:TPU:1, one launch (start us, length us, event | category | flops | bytes accessed | tf_op | source)
XLA Modules:
  0.0 47.1 jit_solution(11944340079274054576)
XLA Ops:
  1.3 43.6 %flow.1 = (f32[8,128]{1,0:T(8,128)}, f32[2,16,128]{2,1,0:T(8,128)}) custom-call(bf16[2,4,64,128]{3,2,1,0:T(8,128)(2,1)} %bitcast.7, bf16[2,4,64,128]{3,2,1,0:T(8,128)(2,1)} %bitcast.8, bf16[16,128,128]{2,1,0:T(8,128)(2,1)} %f1.1, bf16[16,128,128]{2,1,0:T(8,128)(2,1)} %f2.1, s32[12,1,32]{2,1,0:T(1,128)} %bitcast.9, s32[1,1]{1,0:T(1,128)S(6)} %copy.9.cnt), custom_call_target="tpu_custom_call" | custom-call | tf_op jit(solution)/shard_map/flow/pallas_call | solution.py:352
  44.9 0.8 %reshape.26 = f32[2,2,8,8,16]{4,3,2,1,0:T(8,128)S(1)} reshape(f32[2,16,128]{2,1,0:T(8,128)} %get-tuple-element.5) | data formatting | bytes 32768 | tf_op jit(solution)/shard_map/reshape | solution.py:389
  45.7 0.0 copy-start
  45.7 0.7 %reshape.27 = f32[2,16,128]{2,1,0:T(8,128)} reshape(f32[2,2,8,8,16]{4,3,2,1,0:T(8,128)S(1)} %copy.8) | data formatting | bytes 32768 | tf_op jit(solution)/shard_map/reshape | solution.py:389
  46.4 0.0 copy-done
  46.4 0.7 %reshape.25 = f32[2,8,64]{2,1,0:T(8,128)} reshape(f32[8,128]{1,0:T(8,128)S(1)} %copy-done) | data formatting | bytes 8192 | tf_op jit(solution)/shard_map/reshape | solution.py:388
  (1 shorter events, 0.0 us)
Async XLA Ops:
  45.7 0.7 %copy-start = (f32[8,128]{1,0:T(8,128)S(1)}, f32[8,128]{1,0:T(8,128)}, u32[]{:S(2)}) copy-start(f32[8,128]{1,0:T(8,128)} %get-tuple-element.4) | copy-start | bytes 12292

commit v2 on v1

--- a/solution.py
+++ b/solution.py
@@ -13,6 +13,7 @@
 BF16 = jnp.bfloat16
 NROWS, NCOLS = 8, 32
 NZ = 8
+NH = 2
 CH = 128
 BH, BW = 8, 64
 FH, FW = 16, 128
@@ -35,7 +36,7 @@
 def kernel(
     c1, c2, f1, f2, sel, cnt,
     coarse_out, fine_out,
-    kb, qb, q2, f1v, ext, wbuf, maskb, pscr, selv, cntv, lv, biasb, acc, st_tx, st_rx, fl, ft,
+    kb, qb, q2, f1v, ext, wbuf, maskb, pscr, selv, cntv, lv, biasb, acc, st_tx, st_rx, fl, ft, part_sum,
     ring_send, ring_recv, q_send, q_recv, lv_send, lv_recv, halo_send, halo_recv,
     st_send, st_recv, fl_send, fl_recv, loc,
 ):
@@ -114,7 +115,7 @@
             device_id=ring_to[way], device_id_type=MESH,
         )
 
-    for h in range(2):
+    for h in range(NH):
         for way in range(2):
             ring(way, 0, h, c2.at[h]).start()
 
@@ -125,9 +126,15 @@
         )
 
     lives = [share(j, lv.at[0], lv.at[j], lv_send, lv_recv) for j in (1, 2, 3)]
-    asks = [share(j, c1, qb.at[j], q_send, q_recv) for j in (1, 2, 3)]
-    for copy in asks:
-        copy.start()
+    asks = [share(1, c1, qb.at[1], q_send, q_recv), share(2, c1, qb.at[2], q_send, q_recv)]
+    asks.append(
+        pltpu.make_async_remote_copy(
+            src_ref=qb.at[2], dst_ref=qb.at[3], send_sem=q_send.at[2], recv_sem=q_recv.at[2],
+            device_id=partner(1), device_id_type=MESH,
+        )
+    )
+    asks[1].start()
+    asks[0].start()
 
     own_sel.wait()
     own_cnt.wait()
@@ -154,7 +161,7 @@
 
     key = lax.broadcasted_iota(jnp.int32, (512, 128), 0)
     query = lax.broadcasted_iota(jnp.int32, (512, 128), 1)
-    off_y = key // 32 - RAD - query // 16
+    off_y = key // 32 - RAD - (7 - query // 16)
     off_x = key % 32 - PAD - query % 16
     inside = (jnp.abs(off_y) <= RAD) & (jnp.abs(off_x) <= RAD)
     maskb[...] = jnp.where(inside, 0.0, LOW)
@@ -175,23 +182,11 @@
         high = q.astype(BF16)
         q2[j] = jnp.concatenate([high, (q - high.astype(F32)).astype(BF16)], axis=1)
 
-    set_bias(0)
-    own_q.wait()
-    split(0)
-    own_k.wait()
-    own_f1.wait()
-    own_f2.wait()
-    for j in (1, 2, 3):
-        lives[j - 1].wait_recv()
-        set_bias(j)
-        asks[j - 1].wait_recv()
-        split(j)
-
-    def match(at, panel):
+    def match(at, panel, tiles):
         keys = kb[at].reshape(BH * BW, CH)
         keys = jnp.concatenate([keys, keys], axis=1)
         base = (panel * BW).astype(F32)
-        for j in range(4):
+        for j in tiles:
             for lanes in (pl.ds(0, 256), pl.ds(256, 256)):
                 score = lax.dot_general(keys, q2[j, lanes, :], NT, preferred_element_type=F32)
                 score = score.reshape(64, 8, 256)
@@ -218,7 +213,8 @@
         by, bx = b // 8, b % 8
         rows = pl.ds(by * 8, 16)
         keys = ext[rows, pl.ds(pl.multiple_of(bx * 16, 16), 32), :].reshape(512, CH)
-        queries = f1v[pl.ds(by * 8, 8), pl.ds(pl.multiple_of(bx * 16, 16), 16), :].reshape(128, CH)
+        queries = f1v[pl.ds(by * 8, 8), pl.ds(pl.multiple_of(bx * 16, 16), 16), :]
+        queries = jnp.concatenate([queries[7 - i] for i in range(8)], axis=0)
         score = lax.dot_general(keys, queries, NT, preferred_element_type=F32) + maskb[...]
         top = jnp.max(score, axis=0, keepdims=True)
         weight = jnp.exp2((score - top) * SCALE)
@@ -228,37 +224,56 @@
         pscr[...] = pairs.reshape(256, 128)
         wbuf[b] = pscr[pl.ds(0, 128, stride=2), :] + pscr[pl.ds(1, 128, stride=2), :]
 
-    def ready_windows():
-        each(halos, "wait_recv")
-
     def two_windows(i, _):
         window(2 * i)
         window(2 * i + 1)
         return 0
 
-    def step(p, _):
-        @pl.when(p < 6)
-        def _():
-            d, h = p // 2, p % 2
+    def panel_of(p):
+        depth = (p + 1) // 2
+        sign = jnp.where(p == 7, -1, 1 - 2 * (p % 2))
+        return ylo * 16 + ((z + NZ + sign * depth) % NZ) * 2 + core
+
+    def forward(n):
+        d = n // 2
+        for i in range(NH // 2):
+            h = (n % 2) * (NH // 2) + i
             for way in range(2):
                 ring(way, d, h, kb.at[0, 0]).wait_recv()
 
-                @pl.when((d < 2) | (h == way))
-                def _(way=way):
+                @pl.when((d < 2) | (n % 2 == way))
+                def _(way=way, h=h):
                     ring(way, d + 1, h, kb.at[1 + 2 * d + way, h]).start()
 
-        @pl.when(p == 7)
+    set_bias(0)
+    own_q.wait()
+    split(0)
+    own_k.wait()
+    match(0, panel_of(0), (0,))
+    forward(0)
+    asks[1].wait_recv()
+    asks[2].start()
+    forward(1)
+    for j in (1, 2, 3):
+        lives[j - 1].wait_recv()
+        set_bias(j)
+        if j != 2:
+            asks[j - 1].wait_recv()
+        split(j)
+    match(0, panel_of(0), (1, 2, 3))
+
+    def step(p, _):
+        @pl.when(p < 5)
         def _():
-            for way in range(2):
-                ring(way, 3, way, kb.at[0, 0]).wait_recv()
-
-        depth = (p + 1) // 2
-        sign = jnp.where(p == 7, -1, 1 - 2 * (p % 2))
-        zs = (z + NZ + sign * depth) % NZ
-        match(p, ylo * 16 + zs * 2 + core)
+            forward(p + 1)
+
+        match(p, panel_of(p), (0, 1, 2, 3))
         return 0
 
-    lax.fori_loop(0, 8, step, 0)
+    lax.fori_loop(1, 7, step, 0)
+    for i in range(NH // 2):
+        for way in range(2):
+            ring(way, 3, way * (NH // 2) + i, kb.at[0, 0]).wait_recv()
 
     sub = lax.broadcasted_iota(jnp.int32, (8, 512), 0).astype(F32)
 
@@ -272,10 +287,14 @@
 
     backs = [share(j, st_tx.at[j - 1], st_rx.at[j - 1], st_send, st_recv) for j in (1, 2, 3)]
     for j in (3, 2, 1):
+        match(7, panel_of(7), (j,))
         st_tx[j - 1] = moments(j)
         backs[j - 1].start()
+    match(7, panel_of(7), (0,))
     parts = [moments(0)]
-    ready_windows()
+    own_f1.wait()
+    own_f2.wait()
+    each(halos, "wait_recv")
     lax.fori_loop(0, 4, two_windows, 0)
     for j in (1, 2, 3):
         backs[j - 1].wait_recv()
@@ -292,7 +311,6 @@
     flow_y = (in_row / total - query_row) * (1.0 / 256.0)
     flow = jnp.concatenate([f[:, 128 * i : 128 * i + 128] for f in (flow_x, flow_y) for i in range(4)], axis=0)
     fl[1, 1] = flow
-    coarse_out[...] = flow
     edges = []
     for i, (dy, dx) in enumerate(NEIGHBOURS):
         edges.append(
@@ -303,40 +321,74 @@
             )
         )
     each(edges, "start")
+
+    for k in range(2):
+        for i in range(4):
+            pair = flow[k * 4 + i : k * 4 + i + 1, :]
+            coarse_out[k, 2 * i : 2 * i + 1, :] = pair[:, :BW]
+            coarse_out[k, 2 * i + 1 : 2 * i + 2, :] = pair[:, BW:]
     lax.fori_loop(4, 8, two_windows, 0)
+
+    def spread(k, e, lo, hi, sources):
+        shape = (hi - lo, 128)
+        row = (e - 2) % 8
+        i72 = lax.broadcasted_iota(jnp.int32, shape, 0) + lo
+        lane = lax.broadcasted_iota(jnp.int32, shape, 1)
+        goal = jnp.where(i72 < 4, 60 + i72, jnp.where(i72 < 68, i72 - 4, i72 - 68)) + (row % 2) * 64
+        at = k * 4 + row // 2
+        left, mid, right = (s[at : at + 1, :] for s in sources)
+        pick = jnp.where(i72 < 4, left, jnp.where(i72 < 68, mid, right))
+        value = jnp.sum(jnp.where(lane == goal, pick, 0.0), axis=1, keepdims=True)
+        ft[k, e, lo:hi, :] = jnp.broadcast_to(value, shape)
+
+    def weighed(k, b, rows, lo, hi):
+        by, bx = b // 8, b % 8
+        weight = wbuf[b].reshape(8, 16, 128)[rows.start : rows.stop, lo:hi]
+        value = ft[k, by * 4 + rows.start : by * 4 + rows.stop, bx * 8 + lo : bx * 8 + hi, :]
+        terms = (weight * value).reshape(-1, 8, 128)
+        return functools.reduce(jnp.add, [terms[i] for i in range(terms.shape[0])])
+
+    def inner(b):
+        by, bx = b // 8, b % 8
+        return (range(2, 8) if by == 0 else range(0, 6)), (8 if bx == 0 else 0), (8 if bx == 7 else 16)
+
+    for k in range(2):
+        for e in range(2, 10):
+            spread(k, e, 8, 64, (flow, flow, flow))
+        for b in range(16):
+            part_sum[k, b] = weighed(k, b, *inner(b))
+
     each(edges, "wait_recv")
-
-    tiles = {}
-    for ty in range(3):
-        for tx in range(3):
-            tiles[ty, tx] = fl[ty, tx]
-
-    i72 = lax.broadcasted_iota(jnp.int32, (72, 128), 0)
-    lane = lax.broadcasted_iota(jnp.int32, (72, 128), 1)
-    goal = jnp.where(i72 < 4, 60 + i72, jnp.where(i72 < 68, i72 - 4, i72 - 68))
-    for e in range(12):
-        ty = 0 if e < 2 else (1 if e < 10 else 2)
-        row = (e - 2) % 8
-        hit = lane == goal + (row % 2) * 64
-        for k in range(2):
-            at = k * 4 + row // 2
-            left, mid, right = (tiles[ty, tx][at : at + 1, :] for tx in range(3))
-            pick = jnp.where(i72 < 4, left, jnp.where(i72 < 68, mid, right))
-            ft[k, e] = jnp.broadcast_to(
-                jnp.sum(jnp.where(hit, pick, 0.0), axis=1, keepdims=True), (72, 128)
-            )
-
-    for b in range(16):
-        by, bx = b // 8, b % 8
-        weight = wbuf[b].reshape(8, 16, 128)
-        for k in range(2):
-            value = ft[k, by * 4 : by * 4 + 8, bx * 8 : bx * 8 + 16, :]
-            fine_out[k, b : b + 1, :] = jnp.sum((weight * value).reshape(128, 128), axis=0, keepdims=True)
-
-    for h in range(2):
+    for k in range(2):
+        for e in range(12):
+            sources = [fl[0 if e < 2 else (1 if e < 10 else 2), tx] for tx in range(3)]
+            if 2 <= e < 10:
+                spread(k, e, 0, 8, sources)
+                spread(k, e, 64, 72, sources)
+            else:
+                spread(k, e, 0, 72, sources)
+    lane8 = lax.broadcasted_iota(jnp.int32, (8, 128), 1)
+    sub8 = lax.broadcasted_iota(jnp.int32, (8, 128), 0)
+    for k in range(2):
+        for by in range(2):
+            band = jnp.zeros((8, 128), F32)
+            for bx in range(8):
+                b = by * 8 + bx
+                rows, lo, hi = inner(b)
+                value = part_sum[k, b] + weighed(k, b, range(0, 2) if by == 0 else range(6, 8), 0, 16)
+                if lo:
+                    value = value + weighed(k, b, rows, 0, lo)
+                if hi < 16:
+                    value = value + weighed(k, b, rows, hi, 16)
+                value = jnp.broadcast_to(jnp.sum(value, axis=0, keepdims=True), (8, 128))
+                value = pltpu.roll(value, (bx * 16 + 16) % 128, 1)
+                band = jnp.where((lane8 // 16 + sub8) % 8 == bx, value, band)
+            fine_out[k, by * 8 : by * 8 + 8, :] = pltpu.roll(band, 0, 1, stride=16, stride_axis=0)
+
+    for h in range(NH):
         for way in range(2):
             for d in range(4):
-                if d < 3 or h == way:
+                if d < 3 or h // (NH // 2) == way:
                     ring(way, d, h, kb.at[0, 0]).wait_send()
     for copy in asks + lives + backs:
         copy.wait_send()
@@ -351,11 +403,11 @@
     vm_spec = pl.BlockSpec(memory_space=pltpu.VMEM)
     coarse, fine = pl.pallas_call(
         kernel,
-        out_shape=(jax.ShapeDtypeStruct((8, 128), F32), jax.ShapeDtypeStruct((2, 16, 128), F32)),
+        out_shape=(jax.ShapeDtypeStruct((2, BH, BW), F32), jax.ShapeDtypeStruct((2, FH, FW), F32)),
         in_specs=[any_spec] * 5 + [pl.BlockSpec(memory_space=pltpu.HBM)],
         out_specs=(vm_spec, vm_spec),
         scratch_shapes=[
-            vm((8, 2, 4, BW, CH), BF16),
+            vm((8, NH, BH // NH, BW, CH), BF16),
             vm((4, 2, 4, BW, CH), BF16),
             vm((4, BH * BW, 2 * CH), BF16),
             vm((FH, FW, CH), BF16),
@@ -372,7 +424,8 @@
             vm((3, 8, 512), F32),
             vm((3, 3, 8, 128), F32),
             vm((2, 12, 72, 128), F32),
-            dma((2, 4, 2)), dma((2, 4, 2)),
+            vm((2, 16, 8, 128), F32),
+            dma((2, 4, NH)), dma((2, 4, NH)),
             dma((3,)), dma((3,)), dma((3,)), dma((3,)),
             dma((8,)), dma((8,)),
             dma((3,)), dma((3,)),
@@ -382,11 +435,9 @@
         compiler_params=pltpu.CompilerParams(collective_id=0, has_side_effects=True, vmem_limit_bytes=63 << 20),
         name="flow",
     )(
-        coarse_one.reshape(2, 4, BW, CH), coarse_two.reshape(2, 4, BW, CH), fine_one, fine_two,
+        coarse_one.reshape(2, 4, BW, CH), coarse_two.reshape(NH, BH // NH, BW, CH), fine_one, fine_two,
         selection.reshape(12, 1, NCOLS), counts
     )
-    coarse = coarse.reshape(2, BH, BW)
-    fine = fine.reshape(2, 2, 8, 8, 16).transpose(0, 1, 3, 2, 4).reshape(2, FH, FW)
     return coarse, fine
 
 

time: 47.3 us -> 41.4 us (0.88)
  Pallas kernels: 43.6 us -> 38.1 us
    pallas_call x1, Pallas kernels: 43.6 us -> 38.1 us  [local(): pl.pallas_call(kernel, out_shape=(jax.ShapeDtypeStruct((2, BH, BW), F32),...]
    reshape x3 -> x0, local copies, waits for them, and re-layouts: 2.18 us -> none  [the longest x2 1.51 us: local(): fine.reshape(2, 2, 8, 8, 16).transpose(0, 1, 3, 2, 4).reshape(2, FH, FW)]
    unnamed x2 -> x4, local copies, waits for them, and re-layouts: 0.01 us -> 1.91 us
where the time goes in v2:
time: 41.4 us; the launch traced here: 41.3 us
  Pallas kernels  38.1 us (92%)
  local copies, waits for them, and re-layouts  1.91 us (5%)
  between operations  1.29 us (3%)
    pallas_call x1, Pallas kernels, local(): pl.pallas_call(kernel, out_shape=(jax.ShapeDtypeStruct((2, BH, BW), F32),...  38.1 us
    unnamed x4, local copies, waits for them, and re-layouts  1.91 us

profile of v2, /device:TPU:1, one launch (start us, length us, event | category | flops | bytes accessed | tf_op | source)
XLA Modules:
  0.0 41.3 jit_solution(11867430484819008114)
XLA Ops:
  1.3 38.1 %flow.1 = (f32[2,8,64]{2,1,0:T(8,128)}, f32[2,16,128]{2,1,0:T(8,128)}) custom-call(bf16[2,4,64,128]{3,2,1,0:T(8,128)(2,1)} %bitcast.3, bf16[2,4,64,128]{3,2,1,0:T(8,128)(2,1)} %bitcast.4, bf16[16,128,128]{2,1,0:T(8,128)(2,1)} %f1.1, bf16[16,128,128]{2,1,0:T(8,128)(2,1)} %f2.1, s32[12,1,32]{2,1,0:T(1,128)} %bitcast.5, s32[1,1]{1,0:T(1,128)S(6)} %copy.10.cnt), custom_call_target="tpu_custom_call" | custom-call | tf_op jit(solution)/shard_map/flow/pallas_call | solution.py:404
  39.3 0.0 copy-start
  39.4 1.3 %copy.11 = f32[2,8,64]{2,1,0:T(8,128)} copy(f32[2,8,64]{2,1,0:T(8,128)} %get-tuple-element.4) | data formatting | bytes 8192
  40.7 0.0 copy-done
  40.7 0.6 %copy.12 = f32[2,16,128]{2,1,0:T(8,128)} copy(f32[2,16,128]{2,1,0:T(8,128)S(1)} %copy-done) | data formatting | bytes 32768
Async XLA Ops:
  39.3 1.3 %copy-start = (f32[2,16,128]{2,1,0:T(8,128)S(1)}, f32[2,16,128]{2,1,0:T(8,128)}, u32[]{:S(2)}) copy-start(f32[2,16,128]{2,1,0:T(8,128)} %get-tuple-element.5) | copy-start | bytes 49156

commit v3 on v2

--- a/solution.py
+++ b/solution.py
@@ -76,6 +76,27 @@
 
     everyone = list(ring_to) + [partner(j) for j in (1, 2, 3)] + [neighbour(*n) for n in NEIGHBOURS]
 
+    fl[...] = jnp.zeros((3, 3, 8, 128), F32)
+
+    @pl.when(r == 0)
+    def _():
+        ext[0:RAD] = jnp.zeros((RAD, FW + 2 * PAD, CH), BF16)
+
+    @pl.when(r == NROWS - 1)
+    def _():
+        ext[RAD + FH :] = jnp.zeros((RAD, FW + 2 * PAD, CH), BF16)
+
+    @pl.when(c == 0)
+    def _():
+        ext[:, 0:PAD] = jnp.zeros((FH + 2 * RAD, PAD, CH), BF16)
+
+    @pl.when(c == NCOLS - 1)
+    def _():
+        ext[:, PAD + FW :] = jnp.zeros((FH + 2 * RAD, PAD, CH), BF16)
+
+    barrier = pltpu.get_barrier_semaphore()
+    for device in everyone:
+        pl.semaphore_signal(barrier, inc=1, device_id=device, device_id_type=MESH)
     own_sel = pltpu.make_async_copy(sel, selv, loc.at[4])
     own_cnt = pltpu.make_async_copy(cnt, cntv, loc.at[5])
     own_k = pltpu.make_async_copy(c2, kb.at[0], loc.at[0])
@@ -85,27 +106,6 @@
     for copy in (own_sel, own_cnt, own_k, own_q, own_f1, own_f2):
         copy.start()
 
-    fl[...] = jnp.zeros((3, 3, 8, 128), F32)
-
-    @pl.when(r == 0)
-    def _():
-        ext[0:RAD] = jnp.zeros((RAD, FW + 2 * PAD, CH), BF16)
-
-    @pl.when(r == NROWS - 1)
-    def _():
-        ext[RAD + FH :] = jnp.zeros((RAD, FW + 2 * PAD, CH), BF16)
-
-    @pl.when(c == 0)
-    def _():
-        ext[:, 0:PAD] = jnp.zeros((FH + 2 * RAD, PAD, CH), BF16)
-
-    @pl.when(c == NCOLS - 1)
-    def _():
-        ext[:, PAD + FW :] = jnp.zeros((FH + 2 * RAD, PAD, CH), BF16)
-
-    barrier = pltpu.get_barrier_semaphore()
-    for device in everyone:
-        pl.semaphore_signal(barrier, inc=1, device_id=device, device_id_type=MESH)
     pl.semaphore_wait(barrier, len(everyone))
 
     def ring(way, d, h, source):
@@ -157,7 +157,6 @@
                 device_id=neighbour(dy, dx), device_id_type=MESH,
             )
         )
-    each(halos, "start")
 
     key = lax.broadcasted_iota(jnp.int32, (512, 128), 0)
     query = lax.broadcasted_iota(jnp.int32, (512, 128), 1)
@@ -254,13 +253,14 @@
     asks[1].wait_recv()
     asks[2].start()
     forward(1)
+    each(halos, "start")
     for j in (1, 2, 3):
         lives[j - 1].wait_recv()
         set_bias(j)
         if j != 2:
             asks[j - 1].wait_recv()
         split(j)
-    match(0, panel_of(0), (1, 2, 3))
+        match(0, panel_of(0), (j,))
 
     def step(p, _):
         @pl.when(p < 5)
@@ -432,7 +432,7 @@
             dma((8,)), dma((8,)),
             dma((6,)),
         ],
-        compiler_params=pltpu.CompilerParams(collective_id=0, has_side_effects=True, vmem_limit_bytes=63 << 20),
+        compiler_params=pltpu.CompilerParams(collective_id=0, has_side_effects=True, vmem_limit_bytes=55136 << 10),
         name="flow",
     )(
         coarse_one.reshape(2, 4, BW, CH), coarse_two.reshape(NH, BH // NH, BW, CH), fine_one, fine_two,

time: 41.4 us -> 38.8 us (0.937); the launches traced: 41.3 us -> 38.2 us
  Pallas kernels: 38.1 us -> 35.6 us
  local copies, waits for them, and re-layouts: 1.91 us -> 1.23 us
    pallas_call x1, Pallas kernels: 38.1 us -> 35.6 us  [local(): pl.pallas_call(kernel, out_shape=(jax.ShapeDtypeStruct((2, BH, BW), F32),...]
    unnamed x4, local copies, waits for them, and re-layouts: 1.91 us -> 1.23 us
where the time goes in v3:
time: 38.8 us; the launch traced here: 38.2 us
  Pallas kernels  35.6 us (92%)
  between operations  1.31 us (3%)
  local copies, waits for them, and re-layouts  1.23 us (3%)
    pallas_call x1, Pallas kernels, local(): pl.pallas_call(kernel, out_shape=(jax.ShapeDtypeStruct((2, BH, BW), F32),...  35.6 us
    unnamed x4, local copies, waits for them, and re-layouts  1.23 us

profile of v3, /device:TPU:1, one launch (start us, length us, event | category | flops | bytes accessed | tf_op | source)
XLA Modules:
  0.0 38.2 jit_solution(6763912396369085267)
XLA Ops:
  0.6 0.0 copy-start
  1.3 0.0 copy-done
  1.3 35.6 %flow.1 = (f32[2,8,64]{2,1,0:T(8,128)S(1)}, f32[2,16,128]{2,1,0:T(8,128)S(1)}) custom-call(bf16[2,4,64,128]{3,2,1,0:T(8,128)(2,1)} %bitcast.4, bf16[2,4,64,128]{3,2,1,0:T(8,128)(2,1)} %bitcast.5, bf16[16,128,128]{2,1,0:T(8,128)(2,1)} %f1.1, bf16[16,128,128]{2,1,0:T(8,128)(2,1)} %f2.1, s32[12,1,32]{2,1,0:T(1,128)S(1)} %bitcast.3, s32[1,1]{1,0:T(1,128)S(6)} %copy.10.cnt), custom_call_target="tpu_custom_call" | custom-call | tf_op jit(solution)/shard_map/flow/pallas_call | solution.py:404
  37.0 0.6 %copy.11 = f32[2,8,64]{2,1,0:T(8,128)} copy(f32[2,8,64]{2,1,0:T(8,128)S(1)} %get-tuple-element.4) | data formatting | bytes 8192
  37.6 0.6 %copy.12 = f32[2,16,128]{2,1,0:T(8,128)} copy(f32[2,16,128]{2,1,0:T(8,128)S(1)} %get-tuple-element.5) | data formatting | bytes 32768
Async XLA Ops:
  0.6 0.7 %copy-start = (s32[1,1,12,32]{3,1,2,0:T(1,128)S(1)}, s32[1,1,12,32]{3,1,2,0:T(1,128)}, u32[]{:S(2)}) copy-start(s32[1,1,12,32]{3,1,2,0:T(1,128)} %param.10) | copy-start | bytes 4612

commit v4 on v3

--- a/solution.py
+++ b/solution.py
@@ -13,7 +13,8 @@
 BF16 = jnp.bfloat16
 NROWS, NCOLS = 8, 32
 NZ = 8
-NH = 2
+GROUP = 4
+NH = 4
 CH = 128
 BH, BW = 8, 64
 FH, FW = 16, 128
@@ -115,7 +116,7 @@
             device_id=ring_to[way], device_id_type=MESH,
         )
 
-    for h in range(NH):
+    for h in range(NH // 2):
         for way in range(2):
             ring(way, 0, h, c2.at[h]).start()
 
@@ -208,7 +209,7 @@
                 acc[j, 2, :, lanes] = keep * acc[j, 2, :, lanes] + take * in_col
                 acc[j, 3, :, lanes] = keep * acc[j, 3, :, lanes] + take * in_row
 
-    def window(b):
+    def window(b, buffer):
         by, bx = b // 8, b % 8
         rows = pl.ds(by * 8, 16)
         keys = ext[rows, pl.ds(pl.multiple_of(bx * 16, 16), 32), :].reshape(512, CH)
@@ -220,12 +221,12 @@
         total = jnp.sum(weight, axis=0, keepdims=True)
         pairs = weight.reshape(8, 2, 32, 128)
         pairs = (pairs[:, 0] + pairs[:, 1]) * (1.0 / total)
-        pscr[...] = pairs.reshape(256, 128)
-        wbuf[b] = pscr[pl.ds(0, 128, stride=2), :] + pscr[pl.ds(1, 128, stride=2), :]
-
-    def two_windows(i, _):
-        window(2 * i)
-        window(2 * i + 1)
+        pscr[buffer] = pairs.reshape(256, 128)
+        wbuf[b] = pscr[buffer, pl.ds(0, 128, stride=2), :] + pscr[buffer, pl.ds(1, 128, stride=2), :]
+
+    def some_windows(i, _):
+        for n in range(GROUP):
+            window(GROUP * i + n, n)
         return 0
 
     def panel_of(p):
@@ -249,6 +250,9 @@
     split(0)
     own_k.wait()
     match(0, panel_of(0), (0,))
+    for h in range(NH // 2, NH):
+        for way in range(2):
+            ring(way, 0, h, c2.at[h]).start()
     forward(0)
     asks[1].wait_recv()
     asks[2].start()
@@ -295,7 +299,7 @@
     own_f1.wait()
     own_f2.wait()
     each(halos, "wait_recv")
-    lax.fori_loop(0, 4, two_windows, 0)
+    lax.fori_loop(0, 8 // GROUP, some_windows, 0)
     for j in (1, 2, 3):
         backs[j - 1].wait_recv()
         parts.append(st_rx[j - 1])
@@ -327,7 +331,7 @@
             pair = flow[k * 4 + i : k * 4 + i + 1, :]
             coarse_out[k, 2 * i : 2 * i + 1, :] = pair[:, :BW]
             coarse_out[k, 2 * i + 1 : 2 * i + 2, :] = pair[:, BW:]
-    lax.fori_loop(4, 8, two_windows, 0)
+    lax.fori_loop(8 // GROUP, 16 // GROUP, some_windows, 0)
 
     def spread(k, e, lo, hi, sources):
         shape = (hi - lo, 128)
@@ -414,7 +418,7 @@
             vm((FH + 2 * RAD, FW + 2 * PAD, CH), BF16),
             vm((16, 128, 128), F32),
             vm((512, 128), F32),
-            vm((256, 128), F32),
+            vm((GROUP, 256, 128), F32),
             vm((12, 1, NCOLS), jnp.int32),
             vm((1, 1), jnp.int32),
             vm((4, 8, 128), F32),

time: 38.8 us -> 38.4 us (0.990)
  the two profiles are of different devices: /device:TPU:1 before, /device:TPU:7 now
where the time goes in v4:
time: 38.4 us; the launch traced here: 38.3 us
  Pallas kernels  35.8 us (93%)
  between operations  1.31 us (3%)
  local copies, waits for them, and re-layouts  1.23 us (3%)
    pallas_call x1, Pallas kernels, local(): pl.pallas_call(kernel, out_shape=(jax.ShapeDtypeStruct((2, BH, BW), F32),...  35.8 us
    unnamed x4, local copies, waits for them, and re-layouts  1.23 us

profile of v4, /device:TPU:7, one launch (start us, length us, event | category | flops | bytes accessed | tf_op | source)
XLA Modules:
  0.0 38.3 jit_solution(898950377505290587)
XLA Ops:
  0.6 0.0 copy-start
  1.3 0.0 copy-done
  1.3 35.8 %flow.1 = (f32[2,8,64]{2,1,0:T(8,128)S(1)}, f32[2,16,128]{2,1,0:T(8,128)S(1)}) custom-call(bf16[2,4,64,128]{3,2,1,0:T(8,128)(2,1)} %bitcast.4, bf16[4,2,64,128]{3,2,1,0:T(8,128)(2,1)} %bitcast.5, bf16[16,128,128]{2,1,0:T(8,128)(2,1)} %f1.1, bf16[16,128,128]{2,1,0:T(8,128)(2,1)} %f2.1, s32[12,1,32]{2,1,0:T(1,128)S(1)} %bitcast.3, s32[1,1]{1,0:T(1,128)S(6)} %copy.10.cnt), custom_call_target="tpu_custom_call" | custom-call | tf_op jit(solution)/shard_map/flow/pallas_call | solution.py:408
  37.1 0.6 %copy.11 = f32[2,8,64]{2,1,0:T(8,128)} copy(f32[2,8,64]{2,1,0:T(8,128)S(1)} %get-tuple-element.4) | data formatting | bytes 8192
  37.7 0.6 %copy.12 = f32[2,16,128]{2,1,0:T(8,128)} copy(f32[2,16,128]{2,1,0:T(8,128)S(1)} %get-tuple-element.5) | data formatting | bytes 32768
Async XLA Ops:
  0.6 0.7 %copy-start = (s32[1,1,12,32]{3,1,2,0:T(1,128)S(1)}, s32[1,1,12,32]{3,1,2,0:T(1,128)}, u32[]{:S(2)}) copy-start(s32[1,1,12,32]{3,1,2,0:T(1,128)} %param.10) | copy-start | bytes 4612

commit v5 on v4

--- a/solution.py
+++ b/solution.py
@@ -22,7 +22,7 @@
 PAD = 8
 SCALE = float(np.log2(np.e) / np.sqrt(128.0))
 LOW = -1.0e30
-NEIGHBOURS = [(dy, dx) for dy in (-1, 0, 1) for dx in (-1, 0, 1) if (dy, dx) != (0, 0)]
+NEIGHBOURS = [(dy, dx) for dy in (-1, 1, 0) for dx in (-1, 0, 1) if (dy, dx) != (0, 0)]
 NT = (((1,), (1,)), ((), ()))
 
 
@@ -299,7 +299,7 @@
     own_f1.wait()
     own_f2.wait()
     each(halos, "wait_recv")
-    lax.fori_loop(0, 8 // GROUP, some_windows, 0)
+    lax.fori_loop(0, 4 // GROUP, some_windows, 0)
     for j in (1, 2, 3):
         backs[j - 1].wait_recv()
         parts.append(st_rx[j - 1])
@@ -331,7 +331,7 @@
             pair = flow[k * 4 + i : k * 4 + i + 1, :]
             coarse_out[k, 2 * i : 2 * i + 1, :] = pair[:, :BW]
             coarse_out[k, 2 * i + 1 : 2 * i + 2, :] = pair[:, BW:]
-    lax.fori_loop(8 // GROUP, 16 // GROUP, some_windows, 0)
+    lax.fori_loop(4 // GROUP, 16 // GROUP, some_windows, 0)
 
     def spread(k, e, lo, hi, sources):
         shape = (hi - lo, 128)

time: 38.4 us -> 38.4 us (level)
  no operation moved by 1% of the time
where the time goes in v5:
time: 38.4 us; the launch traced here: 38.3 us
  Pallas kernels  35.8 us (93%)
  between operations  1.31 us (3%)
  local copies, waits for them, and re-layouts  1.23 us (3%)
    pallas_call x1, Pallas kernels, local(): pl.pallas_call(kernel, out_shape=(jax.ShapeDtypeStruct((2, BH, BW), F32),...  35.8 us
    unnamed x4, local copies, waits for them, and re-layouts  1.23 us

profile of v5, /device:TPU:7, one launch (start us, length us, event | category | flops | bytes accessed | tf_op | source)
XLA Modules:
  0.0 38.3 jit_solution(5389194166424155942)
XLA Ops:
  0.6 0.0 copy-start
  1.3 0.0 copy-done
  1.3 35.8 %flow.1 = (f32[2,8,64]{2,1,0:T(8,128)S(1)}, f32[2,16,128]{2,1,0:T(8,128)S(1)}) custom-call(bf16[2,4,64,128]{3,2,1,0:T(8,128)(2,1)} %bitcast.4, bf16[4,2,64,128]{3,2,1,0:T(8,128)(2,1)} %bitcast.5, bf16[16,128,128]{2,1,0:T(8,128)(2,1)} %f1.1, bf16[16,128,128]{2,1,0:T(8,128)(2,1)} %f2.1, s32[12,1,32]{2,1,0:T(1,128)S(1)} %bitcast.3, s32[1,1]{1,0:T(1,128)S(6)} %copy.10.cnt), custom_call_target="tpu_custom_call" | custom-call | tf_op jit(solution)/shard_map/flow/pallas_call | solution.py:408
  37.1 0.6 %copy.11 = f32[2,8,64]{2,1,0:T(8,128)} copy(f32[2,8,64]{2,1,0:T(8,128)S(1)} %get-tuple-element.4) | data formatting | bytes 8192
  37.7 0.6 %copy.12 = f32[2,16,128]{2,1,0:T(8,128)} copy(f32[2,16,128]{2,1,0:T(8,128)S(1)} %get-tuple-element.5) | data formatting | bytes 32768
Async XLA Ops:
  0.6 0.7 %copy-start = (s32[1,1,12,32]{3,1,2,0:T(1,128)S(1)}, s32[1,1,12,32]{3,1,2,0:T(1,128)}, u32[]{:S(2)}) copy-start(s32[1,1,12,32]{3,1,2,0:T(1,128)} %param.10) | copy-start | bytes 4612
